TPU v7x, 256 devices: a whole 4x4x8 slice. The times are simulated.
256 devices in a mesh: dp: 16 (over y, x_hi, core), seq: 16 (over x_lo, z).
Axes of the slice: x: 4 (x_hi: 2, x_lo: 2; x = x_hi * 2 + x_lo), y: 4, z: 8, core: 2. Of those that a mesh axis runs over, the one named last changes fastest.
Arguments:
- stored: bfloat16 [16, 2048, 6144], P('dp', 'seq'), may hold values from -6 to 6
- source_row: int32 [16, 256, 1], P(None, 'seq'), may hold values from 0 to 15; in each aligned block of 16 rows (0 to 15, 16 to 31, ..., all dimensions but the last counted through in order) at most 2 rows name the same one
- source_span: int32 [16, 256], P(None, 'seq'), may hold values from 0 to 15
- segments: int32 [16, 2048], P('dp', 'seq'), may hold values from 0 to 127, never falling along the last dimension, each value on 1 to 256 neighbouring positions
- short_weight: float32 [3, 3, 2048], replicated, may hold values from -3 to 3
- filter_taps: float32 [2048, 2048], P('seq'), may hold values from -2 to 2
- cotangent: bfloat16 [16, 2048, 2048], P('dp', 'seq'), may hold values from -6 to 6
Outputs:
- mixed: bfloat16 [16, 2048, 2048], P('dp', 'seq')
- grad_stored: bfloat16 [16, 2048, 6144], P('dp', 'seq')
- grad_filter: float32 [2048, 2048], P('seq')
- grad_short: float32 [3, 3, 2048], replicated
Inputs may be any that keep to these rules, and one draw needn't show every extreme that they name: `source_row`: within the 16 slots of one sequence that share one value of j // 16, no source sequence is named more than 2 times, and some such group names one exactly 2 times.
All inputs are finite; a program needn't handle non-finite values.
Results may differ from a plain program's by a relative error of at most 0.018.
Values may be sent and summed in bfloat16 or wider, within the bound.
No kernel may reach another device: no remote copies, remote signals or barrier semaphores. Data moves between devices by JAX's collectives and lax.ppermute only.
A program may use at most 128 MiB of HBM per device.

v0:
```python
import math

import jax
import jax.numpy as jnp
from jax import lax
from jax.sharding import PartitionSpec as P

MOST = 2


highest = lax.Precision.HIGHEST


def shifted(value, axis, by):
    length = lax.axis_size(axis)
    pairs = [(i, i + by) for i in range(length) if 0 <= i + by < length]
    return lax.ppermute(value, axis, pairs)


def in_one(arrays, axis):
    line, at, finished = (jnp.concatenate([a.reshape(-1) for a in arrays]), 0, [])
    total = lax.psum(line, axis)
    for a in arrays:
        finished.append(total[at : at + a.size].reshape(a.shape))
        at += a.size
    return tuple(finished)


def copy_for_each(value, axis):
    length = lax.axis_size(axis)
    return lax.all_to_all(
        jnp.broadcast_to(value[None], (length, *value.shape)), axis, 0, 0, tiled=True
    )


def of_everyone(value, axis):
    everything = copy_for_each(value, axis)
    return jnp.sum(everything.astype(jnp.float32), axis=0)


def spectral_tables(blocks, block_rows):
    parts = 2 * blocks
    length = parts * block_rows
    half = blocks + 1
    freq = jnp.arange(half, dtype=jnp.int32)[None, :, None]
    start = jnp.arange(blocks, dtype=jnp.int32)[None, None, :]
    inner = jnp.arange(block_rows, dtype=jnp.int32)[:, None, None]
    angle = (freq * (start * block_rows + inner) % length).astype(jnp.float32) * (
        2.0 * math.pi / length
    )
    first_table = jnp.concatenate([jnp.cos(angle), -jnp.sin(angle)], axis=1)
    left = jnp.arange(block_rows, dtype=jnp.int32)[:, None]
    right = jnp.arange(block_rows, dtype=jnp.int32)[None, :]
    small = (left * right % block_rows).astype(jnp.float32) * (2.0 * math.pi / block_rows)
    cos_small = jnp.cos(small)
    sin_small = jnp.sin(small)
    second_table = jnp.stack(
        [jnp.stack([cos_small, sin_small], axis=1), jnp.stack([-sin_small, cos_small], axis=1)],
        axis=0,
    )
    back_table = jnp.stack(
        [jnp.stack([cos_small, -sin_small], axis=1), jnp.stack([sin_small, cos_small], axis=1)],
        axis=0,
    )
    freq_ids = jnp.arange(half, dtype=jnp.int32)
    weights = (
        jnp.where((freq_ids == 0) | (freq_ids == blocks), 1.0, 2.0).astype(jnp.float32) / length
    )
    turned = jnp.transpose(angle, (0, 2, 1))
    last_table = jnp.stack([jnp.cos(turned) * weights, -jnp.sin(turned) * weights], axis=2)
    return (first_table, second_table, back_table, last_table)


def forward_transform(signal, tables, blocks):
    first_table, second_table, back_table, last_table = tables
    block_rows = signal.shape[0] // blocks
    data = signal.reshape(blocks, block_rows, signal.shape[1])
    first = jnp.einsum("qkp,pqc->qkc", first_table, data, precision=highest)
    first = first.reshape(block_rows, 2, first.shape[1] // 2, signal.shape[1])
    return jnp.einsum("smtq,qtkc->smkc", second_table, first, precision=highest)


def inverse_transform(spec, tables, blocks):
    first_table, second_table, back_table, last_table = tables
    section = jnp.einsum("sqtm,tmkc->sqkc", back_table, spec, precision=highest)
    signal = jnp.einsum("qpsk,sqkc->pqc", last_table, section, precision=highest)
    return signal.reshape(blocks * spec.shape[1], spec.shape[3])


def spec_times(left, right, conj_left):
    if conj_left:
        real_part = left[0] * right[0] + left[1] * right[1]
        imag_part = left[0] * right[1] - left[1] * right[0]
    else:
        real_part = left[0] * right[0] - left[1] * right[1]
        imag_part = left[0] * right[1] + left[1] * right[0]
    return jnp.stack([real_part, imag_part], axis=0)


def left_rim(rows, seg_tail):
    return shifted((rows[-2:], seg_tail), "seq", 1)


def short_conv(rows, weights, prev_rows, mask_one, mask_two):
    tok_rows = rows.shape[0]
    extended = jnp.concatenate([prev_rows, rows], axis=0).astype(jnp.float32)
    lag_one = extended[1 : tok_rows + 1] * mask_one
    lag_two = extended[:tok_rows] * mask_two
    hat = weights[0] * extended[2:] + weights[1] * lag_one + weights[2] * lag_two
    return (hat, lag_one, lag_two)


def shards(stored, source_row, source_span, segments, short_weight, filter_taps, cotangent):
    dp_count = lax.axis_size("dp")
    seq_count = lax.axis_size("seq")
    my_dp = lax.axis_index("dp")
    tok_rows = stored.shape[1]
    width = stored.shape[2]
    channels = width // 3
    span_count = source_span.shape[1]
    span_rows = tok_rows // span_count
    slot_ids = jnp.arange(MOST, dtype=jnp.int32)
    span_ids = jnp.arange(span_count, dtype=jnp.int32)
    sources = source_row[:, :, 0]
    mine = (sources == my_dp).astype(jnp.int32)
    earlier = jnp.cumsum(mine, axis=1) - mine
    picked = mine[:, None, :] * (earlier[:, None, :] == slot_ids[None, :, None]).astype(jnp.int32)
    span_hot = (source_span[:, :, None] == span_ids[None, None, :]).astype(jnp.float32)
    select = jnp.einsum("dmj,djk->dmk", picked.astype(jnp.float32), span_hot).reshape(
        dp_count * MOST, span_count
    )
    select = select.astype(jnp.bfloat16)
    my_sources = lax.dynamic_index_in_dim(sources, my_dp, 0, keepdims=False)
    same_source = my_sources[:, None] == my_sources[None, :]
    lower_slot = span_ids[:, None] > span_ids[None, :]
    my_order = jnp.sum((same_source & lower_slot).astype(jnp.int32), axis=1)
    dp_ids = jnp.arange(dp_count, dtype=jnp.int32)
    take = (
        (my_sources[:, None, None] == dp_ids[None, :, None])
        & (my_order[:, None, None] == slot_ids[None, None, :])
    ).astype(jnp.bfloat16)
    take = take.reshape(span_count, dp_count * MOST)
    tap_cols = jnp.transpose(short_weight, (1, 0, 2)).reshape(3, width)
    seg_local = segments[0]
    seg_tail = seg_local[-2:].astype(jnp.bfloat16)
    span_view = stored[0].reshape(span_count, span_rows, width)
    flat = span_view.reshape(span_count, -1)
    sent = jnp.dot(select, flat, preferred_element_type=jnp.float32).astype(jnp.bfloat16)
    received = lax.all_to_all(
        sent.reshape(dp_count, MOST * span_rows, span_view.shape[2]),
        "dp",
        split_axis=0,
        concat_axis=0,
        tiled=True,
    )
    flat = received.reshape(dp_count * MOST, -1)
    rows = jnp.dot(take, flat, preferred_element_type=jnp.float32).astype(jnp.bfloat16)
    gathered = rows.reshape(tok_rows, received.shape[2])
    prev_rows, prev_ids = left_rim(gathered, seg_tail)
    ids_ext = jnp.concatenate([prev_ids.astype(jnp.float32), seg_local.astype(jnp.float32)])
    mask_one = (ids_ext[1 : tok_rows + 1] == ids_ext[2:]).astype(jnp.float32)[:, None]
    mask_two = (ids_ext[:tok_rows] == ids_ext[2:]).astype(jnp.float32)[:, None]
    mask_one, mask_two = (mask_one, mask_two)
    hat, lag_one, lag_two = short_conv(gathered, tap_cols, prev_rows, mask_one, mask_two)
    key_hat = hat[:, :channels]
    value_hat = hat[:, channels : 2 * channels]
    query_hat = hat[:, 2 * channels :]
    product = (key_hat * value_hat).astype(jnp.bfloat16)
    tables = spectral_tables(seq_count, tok_rows)
    filter_cols = lax.all_to_all(filter_taps, "seq", split_axis=1, concat_axis=0, tiled=True)
    mix_cols = lax.all_to_all(product, "seq", split_axis=1, concat_axis=0, tiled=True).astype(
        jnp.float32
    )
    filt_spec = forward_transform(filter_cols, tables, seq_count)
    mix_spec = forward_transform(mix_cols, tables, seq_count)
    conv_cols = inverse_transform(spec_times(filt_spec, mix_spec, False), tables, seq_count)
    conv_rows = lax.all_to_all(
        conv_cols.astype(jnp.bfloat16), "seq", split_axis=0, concat_axis=1, tiled=True
    ).astype(jnp.float32)
    mixed = (query_hat * conv_rows).astype(jnp.bfloat16)
    grad_out = cotangent[0].astype(jnp.float32)
    grad_conv = (grad_out * query_hat).astype(jnp.bfloat16)
    grad_query = grad_out * conv_rows
    cot_cols = lax.all_to_all(grad_conv, "seq", split_axis=1, concat_axis=0, tiled=True).astype(
        jnp.float32
    )
    cot_spec = forward_transform(cot_cols, tables, seq_count)
    back_cols = inverse_transform(spec_times(filt_spec, cot_spec, True), tables, seq_count)
    filter_grad_cols = inverse_transform(spec_times(mix_spec, cot_spec, True), tables, seq_count)
    back_rows = lax.all_to_all(
        back_cols.astype(jnp.bfloat16), "seq", split_axis=0, concat_axis=1, tiled=True
    ).astype(jnp.float32)
    grad_hat = jnp.concatenate([back_rows * value_hat, back_rows * key_hat, grad_query], axis=1)
    values = gathered.astype(jnp.float32)
    tap_terms = jnp.stack(
        [
            jnp.sum(grad_hat * values, axis=0),
            jnp.sum(grad_hat * lag_one, axis=0),
            jnp.sum(grad_hat * lag_two, axis=0),
        ]
    )
    filter_total, taps_dp = tuple(
        (
            part.astype(jnp.float32)
            for part in in_one(
                (filter_grad_cols.astype(jnp.bfloat16), tap_terms.astype(jnp.bfloat16)), "dp"
            )
        )
    )
    taps_total = of_everyone(taps_dp.astype(jnp.bfloat16), "seq").astype(jnp.float32)
    grad_filter = lax.all_to_all(
        filter_total.astype(jnp.bfloat16), "seq", split_axis=0, concat_axis=1, tiled=True
    ).astype(filter_total.dtype)
    grad_short = jnp.transpose(taps_total.reshape(3, 3, channels), (1, 0, 2))
    edge_one = grad_hat * mask_one
    edge_two = grad_hat * mask_two
    next_rows = shifted(
        jnp.concatenate([edge_one[:2], edge_two[:2]], axis=0).astype(jnp.bfloat16), "seq", -1
    ).astype(jnp.float32)
    one_ext = jnp.concatenate([edge_one, next_rows[:2]], axis=0)
    two_ext = jnp.concatenate([edge_two, next_rows[2:]], axis=0)
    grad_rows = (
        tap_cols[0] * grad_hat
        + tap_cols[1] * one_ext[1 : tok_rows + 1]
        + tap_cols[2] * two_ext[2 : tok_rows + 2]
    ).astype(jnp.bfloat16)
    back_send = jnp.dot(
        jnp.transpose(take),
        grad_rows.reshape(span_count, span_rows * width),
        preferred_element_type=jnp.float32,
    ).astype(jnp.bfloat16)
    back_send = back_send.reshape(dp_count, MOST * span_rows, width)
    returned = lax.all_to_all(back_send, "dp", split_axis=0, concat_axis=0, tiled=True)
    grad_stored = jnp.dot(
        jnp.transpose(select),
        returned.reshape(dp_count * MOST, span_rows * width),
        preferred_element_type=jnp.float32,
    ).astype(jnp.bfloat16)
    grad_stored = grad_stored.reshape(1, tok_rows, width)
    return (mixed[None], grad_stored, grad_filter, grad_short)


def solution(mesh):
    return jax.shard_map(
        shards,
        mesh=mesh,
        in_specs=(
            P("dp", "seq", None),
            P(None, "seq", None),
            P(None, "seq"),
            P("dp", "seq"),
            P(),
            P("seq", None),
            P("dp", "seq", None),
        ),
        out_specs=(P("dp", "seq", None), P("dp", "seq", None), P("seq", None), P()),
        check_vma=False,
    )
```

profile of v0, /device:TPU:1, one launch (start us, length us, event | category | flops | bytes accessed | tf_op | source)
XLA Modules:
  0.0 496.2 jit_solution(17421826161161811202)
XLA Ops:
  17.0 8.6 %all-to-all-start = ((bf16[16,16,6144]{2,1,0:T(8,128)(2,1)}), bf16[16,16,6144]{2,1,0:T(8,128)(2,1)}, u32[]{:S(2)}, u32[]{:S(2)}) async-start(bf16[16,16,6144]{2,1,0:T(8,128)(2,1)} %reshape.373), calls=%async_computation | async-start | bytes 6291456 | tf_op jit(solution)/shard_map/all_to_all | solution.py:149
  25.6 3.5 collective-permute-start.1
  35.9 29.4 %all-to-all-done = bf16[16,16,6144]{2,1,0:T(8,128)(2,1)} async-done(((bf16[16,16,6144]{2,1,0:T(8,128)(2,1)}), bf16[16,16,6144]{2,1,0:T(8,128)(2,1)}, u32[]{:S(2)}, u32[]{:S(2)}) %all-to-all-start) | async-done | bytes 3145760 | tf_op jit(solution)/shard_map/all_to_all | solution.py:149
  65.2 8.4 %all-to-all-start.1 = ((f32[128,16,128]{2,0,1:T(8,128)}), f32[128,16,128]{2,0,1:T(8,128)}, u32[]{:S(2)}, u32[]{:S(2)}) async-start(f32[128,16,128]{2,0,1:T(8,128)} %copy.279), calls=%async_computation.1 | async-start | bytes 2097152 | tf_op jit(solution)/shard_map/all_to_all | solution.py:170
  73.6 4.8 reshape.374
  78.5 3.7 convolution_convert_fusion.3
  84.0 3.2 collective-permute-start
  89.3 3.1 collective-permute-done
  96.6 4.8 fusion.6
  104.1 13.6 %all-to-all-start.4 = ((bf16[128,16,128]{2,0,1:T(8,128)(2,1)}), bf16[128,16,128]{2,0,1:T(8,128)(2,1)}, u32[]{:S(2)}, u32[]{:S(2)}) async-start(bf16[128,16,128]{2,0,1:T(8,128)(2,1)} %copy.295), calls=%async_computation.4 | async-start | bytes 1048576 | tf_op jit(solution)/shard_map/all_to_all | solution.py:184
  120.3 6.3 %fusion.78 = f32[128,34,128]{2,1,0:T(8,128)S(1)} fusion(f32[128,34,16]{1,2,0:T(8,128)S(1)} %copy.281, f32[128,16,128]{2,0,1:T(8,128)} %all-to-all-done.1), kind=kOutput, calls=%fused_computation.82 | convolution fusion | flops 106954752 | bytes 3555328 | tf_op jit(solution)/shard_map/qkp,pqc->qkc/dot_general | solution.py:78
  127.0 3.5 fusion.31
  131.2 3.4 fusion.81
  141.6 4.3 fusion.70
  146.1 19.5 %all_to_all.96 = bf16[16,128,128]{2,1,0:T(8,128)(2,1)} all-to-all(bf16[16,128,128]{2,1,0:T(8,128)(2,1)S(1)} %copy.303), channel_id=1, replica_groups=mesh['dp'=16,'seq'=16] {'seq'}, dimensions={0} | all-to-all | bytes 1048576 | tf_op jit(solution)/shard_map/all_to_all | solution.py:190
  167.6 3.3 bitcast_multiply_fusion.2
  173.0 20.0 %all_to_all.97 = bf16[128,16,128]{2,0,1:T(8,128)(2,1)S(1)} all-to-all(bf16[128,16,128]{2,0,1:T(8,128)(2,1)} %copy.284), channel_id=1, replica_groups=mesh['dp'=16,'seq'=16] {'seq'}, dimensions={1} | all-to-all | bytes 1048576 | tf_op jit(solution)/shard_map/all_to_all | solution.py:171
  202.9 4.5 fusion.67
  208.4 6.2 %all-to-all-start.3 = ((bf16[16,128,128]{2,1,0:T(8,128)(2,1)}), bf16[16,128,128]{2,1,0:T(8,128)(2,1)}, u32[]{:S(2)}, u32[]{:S(2)}) async-start(bf16[16,128,128]{2,1,0:T(8,128)(2,1)} %copy.292), calls=%async_computation.3 | async-start | bytes 1048576 | tf_op jit(solution)/shard_map/all_to_all | solution.py:177
  214.6 3.7 fusion.46
  218.4 4.3 fusion.73
  223.6 4.0 all-to-all-done.3
  231.5 9.9 %multiply_reduce_fusion.1 = (bf16[6144]{0:T(1024)(128)(2,1)S(1)}, bf16[6144]{0:T(1024)(128)(2,1)S(1)}, bf16[6144]{0:T(1024)(128)(2,1)S(1)}, f32[128,6144]{0,1:T(8,128)S(1)}, f32[128,6144]{0,1:T(8,128)}) fusion(f32[130,6144]{0,1:T(8,128)} %copy-done, f32[128]{0:T(128)S(1)} %get-tuple-element.69, f32[128,2048]{0,1:T(8,128)} %get-tuple-element.52, ...), kind=kLoop, calls=%fused_computation.27 | loop fusion | flops 10205184 | bytes 17339392 | tf_op jit(solution)/shard_map/reduce_sum | solution.py:198
  246.6 3.2 slice.211
  252.9 130.7 %all-reduce.2.cloned.1.call-done = bf16[280576]{0:T(1024)(128)(2,1)} async-done(((bf16[280576]{0:T(1024)(128)(2,1)}), bf16[280576]{0:T(1024)(128)(2,1)}) %all-reduce.2.cloned.1.call-update) | async-done | bytes 561168 | tf_op jit(solution)/shard_map/psum | solution.py:22
  385.5 6.9 %all-to-all-start.7 = ((bf16[16,128,128]{2,1,0:T(8,128)(2,1)}), bf16[16,128,128]{2,1,0:T(8,128)(2,1)}, u32[]{:S(2)}, u32[]{:S(2)}) async-start(bf16[16,128,128]{2,1,0:T(8,128)(2,1)} %bitcast.181), calls=%async_computation.7 | async-start | bytes 1048576 | tf_op jit(solution)/shard_map/all_to_all | solution.py:211
  396.9 7.3 %all-to-all-done.7 = bf16[16,128,128]{2,1,0:T(8,128)(2,1)} async-done(((bf16[16,128,128]{2,1,0:T(8,128)(2,1)}), bf16[16,128,128]{2,1,0:T(8,128)(2,1)}, u32[]{:S(2)}, u32[]{:S(2)}) %all-to-all-start.7) | async-done | bytes 524320 | tf_op jit(solution)/shard_map/all_to_all | solution.py:211
  405.5 6.7 %all-to-all-start.8 = ((bf16[16,3,6144]{2,1,0:T(4,128)(2,1)}), bf16[16,3,6144]{2,1,0:T(4,128)(2,1)}, u32[]{:S(2)}, u32[]{:S(2)}) async-start(bf16[16,3,6144]{2,1,0:T(4,128)(2,1)} %broadcast_in_dim.16), calls=%async_computation.8 | async-start | bytes 1572864 | tf_op jit(solution)/shard_map/all_to_all | solution.py:31
  412.2 9.7 %fusion.2 = bf16[128,6144]{0,1:T(8,128)(2,1)} fusion(f32[2,6144]{0,1:T(8,128)} %copy.308, f32[128,6144]{0,1:T(8,128)S(1)} %get-tuple-element.47, f32[2,6144]{0,1:T(8,128)} %copy.307, f32[128,6144]{0,1:T(8,128)} %get-tuple-element.48, f32[6144]{0:T(1024)S(1)} %bitcast.186, f32[6144]{0:T(1024)S(1)} %bitcast.188, f32[6144]{0:T(1024)S(1)} %bitcast.184, ...), kind=kLoop, calls=%fused_computation.7 | loop fusion | flops 7864320 | bytes 11182080 | tf_op jit(solution)/shard_map/convert_element_type | solution.py:226
  427.5 2.9 reshape.380
  430.4 11.8 %all-to-all-start.6 = ((bf16[16,16,6144]{2,1,0:T(8,128)(2,1)}), bf16[16,16,6144]{2,1,0:T(8,128)(2,1)S(1)}, u32[]{:S(2)}, u32[]{:S(2)}) async-start(bf16[16,16,6144]{2,1,0:T(8,128)(2,1)} %reshape.380), calls=%async_computation.6 | async-start | bytes 6291456 | tf_op jit(solution)/shard_map/all_to_all | solution.py:233
  453.9 28.0 %all-to-all-done.6 = bf16[16,16,6144]{2,1,0:T(8,128)(2,1)S(1)} async-done(((bf16[16,16,6144]{2,1,0:T(8,128)(2,1)}), bf16[16,16,6144]{2,1,0:T(8,128)(2,1)S(1)}, u32[]{:S(2)}, u32[]{:S(2)}) %all-to-all-start.6) | async-done | bytes 3145760 | tf_op jit(solution)/shard_map/all_to_all | solution.py:233
  (149 shorter events, 97.9 us)
Async XLA Ops:
  7.2 4.3 copy-start.26
  17.0 8.6 %copy-start.25 = (s32[1,128]{1,0:T(1,128)S(1)}, s32[1,128]{1,0:T(1,128)}, u32[]{:S(2)}) copy-start(s32[1,128]{1,0:T(1,128)} %param.10) | copy-start | bytes 1540
  17.0 13.0 %copy-start.15 = (bf16[1,128,2048]{2,1,0:T(8,128)(2,1)S(1)}, bf16[1,128,2048]{2,1,0:T(8,128)(2,1)}, u32[]{:S(2)}) copy-start(bf16[1,128,2048]{2,1,0:T(8,128)(2,1)} %param.13) | copy-start | bytes 1572868
  17.0 48.3 %all-to-all-start = ((bf16[16,16,6144]{2,1,0:T(8,128)(2,1)}), bf16[16,16,6144]{2,1,0:T(8,128)(2,1)}, u32[]{:S(2)}, u32[]{:S(2)}) async-start(bf16[16,16,6144]{2,1,0:T(8,128)(2,1)} %reshape.373), calls=%async_computation | async-start | bytes 6291456 | tf_op jit(solution)/shard_map/all_to_all | solution.py:149
  25.6 10.1 %collective-permute-start.1 = (bf16[2]{0:T(256)(128)(2,1)S(1)}, bf16[2]{0:T(256)(128)(2,1)S(1)}, u32[]{:S(2)}, u32[]{:S(2)}) collective-permute-start(bf16[2]{0:T(256)(128)(2,1)S(1)} %slice_bitcast_fusion), channel_id=1, source_target_pairs={{0,1},{1,2},{2,3},{3,4},{4,5},{5,6},{6,7},{7,8},{8,9},{9,10},{10,1... | collective-permute-start | bytes 20 | tf_op jit(solution)/shard_map/ppermute | solution.py:17
  30.3 71.1 %copy-start.8 = (bf16[1,128,2048]{1,2,0:T(8,128)(2,1)}, bf16[1,128,2048]{1,2,0:T(8,128)(2,1)S(1)}, u32[]{:S(2)}) copy-start(bf16[1,128,2048]{1,2,0:T(8,128)(2,1)S(1)} %copy.294) | copy-start | bytes 1572868
  31.5 4.2 copy-start.22
  35.7 60.8 %copy-start.16 = (f32[1,3,2048]{2,0,1:T(1,128)}, f32[1,3,2048]{2,0,1:T(1,128)S(1)}, u32[]{:S(2)}) copy-start(f32[1,3,2048]{2,0,1:T(1,128)S(1)} %get-tuple-element.58) | copy-start | bytes 73732
  35.8 60.8 %copy-start.18 = (f32[1,3,2048]{2,0,1:T(1,128)}, f32[1,3,2048]{2,0,1:T(1,128)S(1)}, u32[]{:S(2)}) copy-start(f32[1,3,2048]{2,0,1:T(1,128)S(1)} %get-tuple-element.59) | copy-start | bytes 73732
  35.8 60.8 %copy-start.20 = (f32[1,3,2048]{2,0,1:T(1,128)}, f32[1,3,2048]{2,0,1:T(1,128)S(1)}, u32[]{:S(2)}) copy-start(f32[1,3,2048]{2,0,1:T(1,128)S(1)} %get-tuple-element.60) | copy-start | bytes 73732
  65.2 38.9 %all-to-all-start.1 = ((f32[128,16,128]{2,0,1:T(8,128)}), f32[128,16,128]{2,0,1:T(8,128)}, u32[]{:S(2)}, u32[]{:S(2)}) async-start(f32[128,16,128]{2,0,1:T(8,128)} %copy.279), calls=%async_computation.1 | async-start | bytes 2097152 | tf_op jit(solution)/shard_map/all_to_all | solution.py:170
  84.0 3.3 copy-start.7
  84.0 8.4 %collective-permute-start = (bf16[2,6144]{1,0:T(2,128)(2,1)S(1)}, bf16[2,6144]{1,0:T(2,128)(2,1)S(1)}, u32[]{:S(2)}, u32[]{:S(2)}) collective-permute-start(bf16[2,6144]{1,0:T(2,128)(2,1)S(1)} %slice.139), channel_id=1, source_target_pairs={{0,1},{1,2},{2,3},{3,4},{4,5},{5,6},{6,7},{7,8},{8,9},{9,10},{10,1... | collective-permute-start | bytes 73736 | tf_op jit(solution)/shard_map/ppermute | solution.py:17
  87.3 9.2 %copy-start.23 = (f32[128]{0:T(128)}, f32[128]{0:T(128)S(1)}, u32[]{:S(2)}) copy-start(f32[128]{0:T(128)S(1)} %get-tuple-element.70) | copy-start | bytes 1540
  89.3 7.3 %copy-start.6 = (bf16[128,6144]{0,1:T(8,128)(2,1)}, bf16[128,6144]{0,1:T(8,128)(2,1)S(1)}, u32[]{:S(2)}) copy-start(bf16[128,6144]{0,1:T(8,128)(2,1)S(1)} %copy.277) | copy-start | bytes 4718596
  96.5 4.8 copy-start
  101.4 16.3 %copy-start.13 = (f32[128,16,1,17]{0,1,3,2:T(8,128)S(1)}, f32[128,16,1,17]{0,1,3,2:T(8,128)}, u32[]{:S(2)}) copy-start(f32[128,16,1,17]{0,1,3,2:T(8,128)} %get-tuple-element.65) | copy-start | bytes 417796
  101.4 16.3 %copy-start.14 = (f32[128,16,1,17]{0,1,3,2:T(8,128)S(1)}, f32[128,16,1,17]{0,1,3,2:T(8,128)}, u32[]{:S(2)}) copy-start(f32[128,16,1,17]{0,1,3,2:T(8,128)} %get-tuple-element.66) | copy-start | bytes 417796
  104.1 27.1 %all-to-all-start.4 = ((bf16[128,16,128]{2,0,1:T(8,128)(2,1)}), bf16[128,16,128]{2,0,1:T(8,128)(2,1)}, u32[]{:S(2)}, u32[]{:S(2)}) async-start(bf16[128,16,128]{2,0,1:T(8,128)(2,1)} %copy.295), calls=%async_computation.4 | async-start | bytes 1048576 | tf_op jit(solution)/shard_map/all_to_all | solution.py:184
  120.3 6.7 %copy-start.10 = (f32[1,128,2,128]{3,1,2,0:T(8,128)}, f32[1,128,2,128]{3,1,2,0:T(8,128)S(1)}, u32[]{:S(2)}) copy-start(f32[1,128,2,128]{3,1,2,0:T(8,128)S(1)} %get-tuple-element.61) | copy-start | bytes 393220
  135.5 2.6 copy-start.1
  208.4 19.2 %all-to-all-start.3 = ((bf16[16,128,128]{2,1,0:T(8,128)(2,1)}), bf16[16,128,128]{2,1,0:T(8,128)(2,1)}, u32[]{:S(2)}, u32[]{:S(2)}) async-start(bf16[16,128,128]{2,1,0:T(8,128)(2,1)} %copy.292), calls=%async_computation.3 | async-start | bytes 1048576 | tf_op jit(solution)/shard_map/all_to_all | solution.py:177
  214.6 169.0 %all-reduce.2.cloned.1.call-start = ((), (), s32[]{:S(2)}) async-start(), calls=%async_computation.9 | async-start | bytes 1122304 | tf_op jit(solution)/shard_map/psum | solution.py:22
  222.7 6.3 %copy-start.9 = (bf16[1,128,2048]{1,2,0:T(8,128)(2,1)S(1)}, bf16[1,128,2048]{1,2,0:T(8,128)(2,1)}, u32[]{:S(2)}) copy-start(bf16[1,128,2048]{1,2,0:T(8,128)(2,1)} %copy-done.8) | copy-start | bytes 1572868
  223.6 7.9 %copy-start.24 = (f32[128]{0:T(128)S(1)}, f32[128]{0:T(128)}, u32[]{:S(2)}) copy-start(f32[128]{0:T(128)} %copy-done.23) | copy-start | bytes 1540
  251.6 140.8 %collective-permute-start.2 = (bf16[4,6144]{1,0:T(4,128)(2,1)S(1)}, bf16[4,6144]{1,0:T(4,128)(2,1)S(1)}, u32[]{:S(2)}, u32[]{:S(2)}) collective-permute-start(bf16[4,6144]{1,0:T(4,128)(2,1)S(1)} %pad_maximum_fusion.13), channel_id=1, source_target_pairs={{1,0},{2,1},{3,2},{4,3},{5,4},{6,5},{7,6},{8,7},{9,8},{10,9},{11,1... | collective-permute-start | bytes 147464 | tf_op jit(solution)/shard_map/ppermute | solution.py:17
  385.5 18.8 %all-to-all-start.7 = ((bf16[16,128,128]{2,1,0:T(8,128)(2,1)}), bf16[16,128,128]{2,1,0:T(8,128)(2,1)}, u32[]{:S(2)}, u32[]{:S(2)}) async-start(bf16[16,128,128]{2,1,0:T(8,128)(2,1)} %bitcast.181), calls=%async_computation.7 | async-start | bytes 1048576 | tf_op jit(solution)/shard_map/all_to_all | solution.py:211
  394.7 17.4 %copy-start.17 = (f32[1,3,2048]{2,0,1:T(1,128)S(1)}, f32[1,3,2048]{2,0,1:T(1,128)}, u32[]{:S(2)}) copy-start(f32[1,3,2048]{2,0,1:T(1,128)} %copy-done.16) | copy-start | bytes 73732
  394.7 17.5 %copy-start.19 = (f32[1,3,2048]{2,0,1:T(1,128)S(1)}, f32[1,3,2048]{2,0,1:T(1,128)}, u32[]{:S(2)}) copy-start(f32[1,3,2048]{2,0,1:T(1,128)} %copy-done.18) | copy-start | bytes 73732
  394.7 17.5 %copy-start.21 = (f32[1,3,2048]{2,0,1:T(1,128)S(1)}, f32[1,3,2048]{2,0,1:T(1,128)}, u32[]{:S(2)}) copy-start(f32[1,3,2048]{2,0,1:T(1,128)} %copy-done.20) | copy-start | bytes 73732
  405.5 25.0 %all-to-all-start.8 = ((bf16[16,3,6144]{2,1,0:T(4,128)(2,1)}), bf16[16,3,6144]{2,1,0:T(4,128)(2,1)}, u32[]{:S(2)}, u32[]{:S(2)}) async-start(bf16[16,3,6144]{2,1,0:T(4,128)(2,1)} %broadcast_in_dim.16), calls=%async_computation.8 | async-start | bytes 1572864 | tf_op jit(solution)/shard_map/all_to_all | solution.py:31
  430.4 51.4 %all-to-all-start.6 = ((bf16[16,16,6144]{2,1,0:T(8,128)(2,1)}), bf16[16,16,6144]{2,1,0:T(8,128)(2,1)S(1)}, u32[]{:S(2)}, u32[]{:S(2)}) async-start(bf16[16,16,6144]{2,1,0:T(8,128)(2,1)} %reshape.380), calls=%async_computation.6 | async-start | bytes 6291456 | tf_op jit(solution)/shard_map/all_to_all | solution.py:233
  (7 other events, 11.6 us)
Sparse Core Ops, SparseCore 0:
  243.7 139.8 all-reduce.1
where the time goes:
time: 505 us; the launch traced here: 496 us
  waiting for transfers between devices  203 us (40%)
  starting transfers between devices  70.2 us (14%)
  local copies, waits for them, and re-layouts  69 us (14%)
  matrix products  52.5 us (10%)
  other arithmetic  46.5 us (9%)
  blocking collectives  39.5 us (8%)
  between operations  15.2 us (3%)
    psum x1, waiting for transfers between devices, in_one(): total = lax.psum(line, axis)  131 us
    all_to_all x1, waiting for transfers between devices, shards(): lax.all_to_all(sent.reshape(dp_count, MOST * span_rows, span_view.shape[2...  29.4 us
    all_to_all x1, waiting for transfers between devices, shards(): lax.all_to_all(back_send, 'dp', split_axis=0, concat_axis=0, tiled=True)  28 us
    all_to_all x1, blocking collectives, shards(): lax.all_to_all(product, 'seq', split_axis=1, concat_axis=0, tiled=True)  20 us
    all_to_all x1, blocking collectives, shards(): lax.all_to_all(back_cols.astype(jnp.bfloat16), 'seq', split_axis=0, conca...  19.5 us
    all_to_all x1, starting transfers between devices, shards(): lax.all_to_all(grad_conv, 'seq', split_axis=1, concat_axis=0, tiled=True)  13.6 us
    dot_general x3, matrix products, inverse_transform(): jnp.einsum('qpsk,sqkc->pqc', last_table, section, precision=highest)  13.2 us
    dot_general x3, matrix products, forward_transform(): first = jnp.einsum('qkp,pqc->qkc', first_table, data, precision=highest)  12 us
  transfers between devices with their start and end apart: 11, of which 7 were waited for; matrix products, arithmetic and copies ran while one was open for 19% of the time, Pallas kernels for 0%

commit v1 on v0

v1 whole, which is shorter than its diff:
```python
import functools
import math

import jax
import jax.numpy as jnp
import numpy as np
from jax import lax
from jax.experimental import pallas as pl
from jax.experimental.pallas import tpu as pltpu
from jax.sharding import PartitionSpec as P

MOST = 2
CHUNK = 256
LANES = 128
HALO = 8
F32 = jnp.float32
BF16 = jnp.bfloat16


def shifted(value, axis, by):
    length = lax.axis_size(axis)
    pairs = [(i, i + by) for i in range(length) if 0 <= i + by < length]
    return lax.ppermute(value, axis, pairs)


def exchange(value, axis):
    return lax.all_to_all(value, axis, 0, 0, tiled=True)


def dot(left, right):
    return jnp.dot(left, right, preferred_element_type=F32)


def halves(value):
    high = value.astype(BF16)
    return high, (value - high.astype(F32)).astype(BF16)


def dot_three(left_high, left_low, value):
    high, low = halves(value)
    return dot(left_high, high) + (dot(left_high, low) + dot(left_low, high))


def outer_tables():
    blocks = np.arange(16)
    forward = [np.ones(16), np.cos(np.pi * blocks)]
    back = [np.ones(16), np.cos(np.pi * blocks)]
    for k in range(1, 16):
        angle = 2.0 * np.pi * k * blocks / 32.0
        forward += [np.cos(angle), -np.sin(angle)]
        back += [2.0 * np.cos(angle), -2.0 * np.sin(angle)]
    return np.stack(forward), np.stack(back, axis=1) / 4096.0


def numpy_halves(table):
    high = _round(table)
    return high, _round(table - high)


def _round(table):
    return np.asarray(table, np.float32).astype(jnp.bfloat16).astype(np.float64)


def spread(table, by):
    rows, cols = table.shape
    eye = jnp.eye(by, dtype=F32)
    wide = jnp.asarray(table, F32)[:, None, :, None] * eye[None, :, None, :]
    return wide.reshape(rows * by, cols * by).astype(BF16)


def table_kernel(fc_ref, fs_ref, row_ref, col_ref, dh_ref, dl_ref, eh_ref, el_ref):
    fc = fc_ref[...]
    fs = fs_ref[...]

    def put(high_ref, low_ref, r, c, value):
        high, low = halves(value)
        where = (0, pl.ds(r * LANES, LANES), pl.ds(c * LANES, LANES))
        high_ref[where] = high
        low_ref[where] = low

    wc = row_ref[0, 0:1, :]
    ws = row_ref[0, 1:2, :]
    cos = fc * wc - fs * ws
    sin = fs * wc + fc * ws
    put(dh_ref, dl_ref, 0, 0, cos)
    put(dh_ref, dl_ref, 0, 1, sin)
    put(dh_ref, dl_ref, 1, 0, -sin)
    put(dh_ref, dl_ref, 1, 1, cos)
    wc = col_ref[0, :, 0:1]
    ws = col_ref[0, :, 1:2]
    cos = fc * wc - fs * ws
    sin = fs * wc + fc * ws
    put(eh_ref, el_ref, 0, 0, cos)
    put(eh_ref, el_ref, 0, 1, -sin)
    put(eh_ref, el_ref, 1, 0, sin)
    put(eh_ref, el_ref, 1, 1, cos)


def inner_tables():
    inner = jnp.arange(LANES, dtype=jnp.int32)
    turn = (inner[:, None] * inner[None, :] % LANES).astype(F32) * (2.0 * math.pi / LANES)
    order = jnp.asarray([0, 16] + list(range(1, 16)), jnp.int32)
    twist = (order[:, None] * inner[None, :]).astype(F32) * (2.0 * math.pi / 4096)
    rows = jnp.stack([jnp.cos(twist), jnp.sin(twist)], axis=1)
    cols = jnp.stack([jnp.cos(twist), jnp.sin(twist)], axis=2)
    whole = pl.BlockSpec((LANES, LANES), lambda k: (0, 0))
    out = pl.BlockSpec((1, 2 * LANES, 2 * LANES), lambda k: (k, 0, 0))
    shape = jax.ShapeDtypeStruct((17, 2 * LANES, 2 * LANES), BF16)
    return pl.pallas_call(
        table_kernel,
        grid=(17,),
        in_specs=[
            whole,
            whole,
            pl.BlockSpec((1, 2, LANES), lambda k: (k, 0, 0)),
            pl.BlockSpec((1, LANES, 2), lambda k: (k, 0, 0)),
        ],
        out_specs=[out] * 4,
        out_shape=[shape] * 4,
        name="inner_tables",
    )(jnp.cos(turn), jnp.sin(turn), rows, cols)


def gather_kernel(k_ref, v_ref, q_ref, take_ref, pk_ref, pv_ref, pq_ref, mask_ref, w_ref, cot_ref, taps_ref, out_ref, xs):
    take = take_ref[...]
    m1 = mask_ref[0:128, 0:1]
    m2 = mask_ref[0:128, 1:2]
    hats = []
    for s, (ref, prev) in enumerate(((k_ref, pk_ref), (v_ref, pv_ref), (q_ref, pq_ref))):
        x = dot(take, ref[...])
        xs[s, 6:8, :] = prev[...].astype(F32)
        xs[s, 8:136, :] = x
        w = w_ref[:, s, :]
        lag_one = xs[s, 7:135, :] * m1
        lag_two = xs[s, 6:134, :] * m2
        hats.append(w[0:1] * x + w[1:2] * lag_one + w[2:3] * lag_two)
    product = (hats[0] * hats[1]).astype(BF16)
    grad_conv = (cot_ref[...].astype(F32) * hats[2]).astype(BF16)
    filt = taps_ref[...].astype(BF16)
    for h in range(CHUNK // LANES):
        at = slice(h * LANES, (h + 1) * LANES)
        out_ref[h, 0:128, :] = product[:, at]
        out_ref[h, 128:256, :] = grad_conv[:, at]
        out_ref[h, 256:384, :] = filt[:, at]


def stream_specs(rows, chunks):
    return [pl.BlockSpec((rows, CHUNK), lambda c, s=s: (0, s * chunks + c)) for s in range(3)]


def gather_rows(received, take, prev, masks, weights, cot, filter_taps):
    chunks = cot.shape[1] // CHUNK
    per = CHUNK // LANES
    return pl.pallas_call(
        gather_kernel,
        grid=(chunks,),
        in_specs=stream_specs(256, chunks)
        + [pl.BlockSpec((128, 256), lambda c: (0, 0))]
        + stream_specs(2, chunks)
        + [
            pl.BlockSpec((136, 2), lambda c: (0, 0)),
            pl.BlockSpec((3, 3, CHUNK), lambda c: (0, 0, c)),
            pl.BlockSpec((128, CHUNK), lambda c: (0, c)),
            pl.BlockSpec((128, CHUNK), lambda c: (0, c)),
        ],
        out_specs=pl.BlockSpec((per, 384, LANES), lambda c: (c, 0, 0)),
        out_shape=jax.ShapeDtypeStruct((chunks * per, 384, LANES), BF16),
        scratch_shapes=[pltpu.VMEM((3, 136, CHUNK), F32)],
        name="gather_rows",
    )(received, received, received, take, prev, prev, prev, masks, weights, cot, filter_taps)


def conv_kernel(in_ref, dh_ref, dl_ref, eh_ref, el_ref, fh_ref, fl_ref, bh_ref, bl_ref, out_ref, ah, al, zh, zl):
    step = pl.program_id(0)
    wide = 3 * LANES

    @pl.when(step == 0)
    def _():
        nothing = jnp.zeros((LANES, wide), BF16)
        for where in (1, 3):
            ah[where] = nothing
            al[where] = nothing
        for g in range(8):
            at = slice(16 * g, 16 * g + 16)
            data = jnp.concatenate(
                [
                    in_ref[:, 128 * i + 16 * g : 128 * i + 16 * g + 16, :].reshape(256, LANES)
                    for i in range(3)
                ],
                axis=1,
            )
            first = dot(fh_ref[...], data) + dot(fl_ref[...], data)
            high, low = halves(first)
            for ref, value in ((ah, high), (al, low)):
                ref[0, at, :] = value[0:16]
                ref[2, at, :] = value[16:32]
                ref[4:34, at, :] = value[32:512].reshape(30, 16, wide)

    pair = pl.ds(2 * step, 2)
    high = ah[pair].reshape(2 * LANES, wide)
    low = al[pair].reshape(2 * LANES, wide)
    spec = dot(dh_ref[0], high) + (dot(dh_ref[0], low) + dot(dl_ref[0], high))
    xr, xi = spec[:LANES, :LANES], spec[LANES:, :LANES]
    gr, gi = spec[:LANES, LANES : 2 * LANES], spec[LANES:, LANES : 2 * LANES]
    hr, hi = spec[:LANES, 2 * LANES :], spec[LANES:, 2 * LANES :]
    real = jnp.concatenate([hr * xr - hi * xi, hr * gr + hi * gi, xr * gr + xi * gi], axis=1)
    imag = jnp.concatenate([hr * xi + hi * xr, hr * gi - hi * gr, xr * gi - xi * gr], axis=1)
    back = dot_three(eh_ref[0], el_ref[0], jnp.concatenate([real, imag], axis=0))
    high, low = halves(back)
    zh[pair] = high.reshape(2, LANES, wide)
    zl[pair] = low.reshape(2, LANES, wide)

    @pl.when(step == 16)
    def _():
        for g in range(8):
            at = slice(16 * g, 16 * g + 16)

            def picked(ref):
                return jnp.concatenate(
                    [ref[0, at, :], ref[2, at, :], ref[4:34, at, :].reshape(480, wide)], axis=0
                )

            high = picked(zh)
            low = picked(zl)
            last = dot(bh_ref[...], high) + (dot(bh_ref[...], low) + dot(bl_ref[...], high))
            for i in range(3):
                part = last[:, i * LANES : (i + 1) * LANES].reshape(16, 16, LANES)
                out_ref[:, 128 * i + 16 * g : 128 * i + 16 * g + 16, :] = part.astype(BF16)
                if g == 0 and i < 2:
                    lead = part[1:, 0:8, :]
                    lead = jnp.concatenate([lead, jnp.zeros((1, 8, LANES), F32)], axis=0)
                    if i == 0:
                        conv_lead = lead
                    else:
                        both = jnp.concatenate([conv_lead, lead], axis=1)
                        out_ref[:, 384:400, :] = both.astype(BF16)


def conv_all(columns, tables):
    fwd, back = outer_tables()
    fh, fl = (spread(t, 16) for t in numpy_halves(fwd))
    bh, bl = (spread(t, 16) for t in numpy_halves(back))
    table = pl.BlockSpec((1, 2 * LANES, 2 * LANES), lambda k: (k, 0, 0))

    def whole(*shape):
        return pl.BlockSpec(shape, lambda k: (0,) * len(shape))

    return pl.pallas_call(
        conv_kernel,
        grid=(17,),
        in_specs=[whole(16, 384, LANES)]
        + [table] * 4
        + [whole(512, 256), whole(512, 256), whole(256, 512), whole(256, 512)],
        out_specs=whole(16, 400, LANES),
        out_shape=jax.ShapeDtypeStruct((16, 400, LANES), BF16),
        scratch_shapes=[pltpu.VMEM((34, LANES, 3 * LANES), BF16) for _ in range(4)],
        name="conv_all",
    )(columns, *tables, fh, fl, bh, bl)


def back_kernel(
    k_ref, v_ref, q_ref, take_ref, give_ref, pk_ref, pv_ref, pq_ref, nk_ref, nv_ref, nq_ref,
    mask_ref, w_ref, cot_ref, next_cot_ref, conv_ref, mixed_ref, back_ref, taps_ref, xs, one, two,
):
    take = take_ref[...]
    give = give_ref[...]
    m1 = mask_ref[:, 0:1]
    m2 = mask_ref[:, 1:2]
    streams = ((k_ref, pk_ref, nk_ref), (v_ref, pv_ref, nv_ref), (q_ref, pq_ref, nq_ref))
    for s, (ref, prev, after) in enumerate(streams):
        xs[s, 6:8, :] = prev[...].astype(F32)
        xs[s, 8:136, :] = dot(take, ref[...])
        xs[s, 136:144, :] = jnp.zeros((8, CHUNK), F32)
        xs[s, 136:138, :] = after[...].astype(F32)
    for h in range(CHUNK // LANES):
        at = slice(h * LANES, (h + 1) * LANES)
        hats = []
        for s in range(3):
            w = w_ref[:, s, at]
            hats.append(
                w[0:1] * xs[s, 8:144, at]
                + w[1:2] * (xs[s, 7:143, at] * m1)
                + w[2:3] * (xs[s, 6:142, at] * m2)
            )
        tail = conv_ref[h, 384:400, :].astype(F32)
        conv = jnp.concatenate([conv_ref[h, 0:128, :].astype(F32), tail[0:8]], axis=0)
        grad_product = jnp.concatenate([conv_ref[h, 128:256, :].astype(F32), tail[8:16]], axis=0)
        cot = jnp.concatenate([cot_ref[:, at].astype(F32), next_cot_ref[:, at].astype(F32)], axis=0)
        mixed_ref[:, at] = (hats[2] * conv)[0:128].astype(BF16)
        grads = (grad_product * hats[1], grad_product * hats[0], cot * conv)
        for s in range(3):
            w = w_ref[:, s, at]
            grad = grads[s]
            here = grad[0:128]
            one[...] = grad * m1
            two[...] = grad * m2
            taps_ref[3 * s : 3 * s + 1, at] = jnp.sum(here * xs[s, 8:136, at], axis=0, keepdims=True)
            taps_ref[3 * s + 1 : 3 * s + 2, at] = jnp.sum(one[0:128] * xs[s, 7:135, at], axis=0, keepdims=True)
            taps_ref[3 * s + 2 : 3 * s + 3, at] = jnp.sum(two[0:128] * xs[s, 6:134, at], axis=0, keepdims=True)
            rows = w[0:1] * here + w[1:2] * one[1:129] + w[2:3] * two[2:130]
            sent = dot(give, rows.astype(BF16)).astype(BF16)
            back_ref[:, 16 * s : 16 * s + 16, at] = sent.reshape(16, 16, LANES)
        lags = conv_ref[h, 256:384, :].astype(F32).reshape(16, 8, LANES)
        back_ref[:, 48:56, at] = lags.astype(BF16)


def back_rows(received, take, give, prev, after, masks, weights, cot, next_cot, columns):
    channels = cot.shape[1]
    chunks = channels // CHUNK
    per = CHUNK // LANES
    return pl.pallas_call(
        back_kernel,
        grid=(chunks,),
        in_specs=stream_specs(256, chunks)
        + [pl.BlockSpec((128, 256), lambda c: (0, 0)), pl.BlockSpec((256, 128), lambda c: (0, 0))]
        + stream_specs(2, chunks)
        + stream_specs(2, chunks)
        + [
            pl.BlockSpec((136, 2), lambda c: (0, 0)),
            pl.BlockSpec((3, 3, CHUNK), lambda c: (0, 0, c)),
            pl.BlockSpec((128, CHUNK), lambda c: (0, c)),
            pl.BlockSpec((8, CHUNK), lambda c: (0, c)),
            pl.BlockSpec((per, 400, LANES), lambda c: (c, 0, 0)),
        ],
        out_specs=[
            pl.BlockSpec((128, CHUNK), lambda c: (0, c)),
            pl.BlockSpec((16, 56, CHUNK), lambda c: (0, 0, c)),
            pl.BlockSpec((9, CHUNK), lambda c: (0, c)),
        ],
        out_shape=[
            jax.ShapeDtypeStruct((128, channels), BF16),
            jax.ShapeDtypeStruct((16, 56, channels), BF16),
            jax.ShapeDtypeStruct((9, channels), F32),
        ],
        scratch_shapes=[
            pltpu.VMEM((3, 144, CHUNK), F32),
            pltpu.VMEM((136, LANES), F32),
            pltpu.VMEM((136, LANES), F32),
        ],
        name="back_rows",
    )(
        received, received, received, take, give, prev, prev, prev, after, after, after,
        masks, weights, cot, next_cot, columns,
    )


def store_kernel(select_ref, in_ref, out_ref):
    width = in_ref.shape[2]
    out_ref[...] = dot(select_ref[...], in_ref[...].reshape(256, width)).astype(BF16)


def store_grads(select, returned, channels):
    width = 512
    chunks = channels // width
    return pl.pallas_call(
        store_kernel,
        grid=(3, chunks),
        in_specs=[
            pl.BlockSpec((128, 256), lambda s, c: (0, 0)),
            pl.BlockSpec((16, 16, width), lambda s, c: (0, s, c)),
        ],
        out_specs=pl.BlockSpec((128, width), lambda s, c: (0, s * chunks + c)),
        out_shape=jax.ShapeDtypeStruct((128, 3 * channels), BF16),
        name="store_grads",
    )(select, returned)


def total_over(value, axis):
    length = lax.axis_size(axis)
    step = 1
    while step < length:
        value = value + lax.ppermute(value, axis, [(i, i ^ step) for i in range(length)])
        step *= 2
    return value


def shards(stored, source_row, source_span, segments, short_weight, filter_taps, cotangent):
    dp_count = lax.axis_size("dp")
    my_dp = lax.axis_index("dp")
    tok_rows = stored.shape[1]
    width = stored.shape[2]
    channels = width // 3
    span_count = source_span.shape[1]
    span_rows = tok_rows // span_count
    slot_ids = jnp.arange(MOST, dtype=jnp.int32)
    span_ids = jnp.arange(span_count, dtype=jnp.int32)
    sources = source_row[:, :, 0]
    mine = (sources == my_dp).astype(jnp.int32)
    earlier = jnp.cumsum(mine, axis=1) - mine
    picked = mine[:, None, :] * (earlier[:, None, :] == slot_ids[None, :, None]).astype(jnp.int32)
    span_hot = (source_span[:, :, None] == span_ids[None, None, :]).astype(F32)
    select = jnp.einsum("dmj,djk->dmk", picked.astype(F32), span_hot).reshape(dp_count * MOST, span_count)
    my_sources = lax.dynamic_index_in_dim(sources, my_dp, 0, keepdims=False)
    same_source = my_sources[:, None] == my_sources[None, :]
    lower_slot = span_ids[:, None] > span_ids[None, :]
    my_order = jnp.sum((same_source & lower_slot).astype(jnp.int32), axis=1)
    place = my_sources * MOST + my_order
    take = (place[:, None] == jnp.arange(dp_count * MOST, dtype=jnp.int32)[None, :]).astype(F32)

    send_rows = spread(select, span_rows)
    select_rows = spread(jnp.transpose(select), span_rows)
    take_rows = spread(take, span_rows)
    give_rows = spread(jnp.transpose(take), span_rows)

    sent = dot(send_rows, stored[0]).astype(BF16)
    received = exchange(sent.reshape(dp_count, MOST * span_rows, width), "dp")
    received = received.reshape(dp_count * MOST * span_rows, width)

    ids = segments[0] + 1
    before_ids = shifted(ids[-2:], "seq", 1)
    after_ids = shifted(ids[:2], "seq", -1)
    all_ids = jnp.concatenate([before_ids, ids, after_ids])
    masks = jnp.stack(
        [all_ids[1 : tok_rows + 3] == all_ids[2 : tok_rows + 4], all_ids[: tok_rows + 2] == all_ids[2 : tok_rows + 4]],
        axis=1,
    ).astype(F32)
    masks = jnp.pad(masks, ((0, 6), (0, 0)))
    cot = cotangent[0]
    next_cot = jnp.pad(shifted(cot[:2], "seq", -1), ((0, 6), (0, 0)))
    weights = jnp.transpose(short_weight, (1, 0, 2))
    tables = inner_tables()

    last = lax.dynamic_slice(received, (place[-1] * span_rows, 0), (span_rows, width))[-2:]
    first = lax.dynamic_slice(received, (place[0] * span_rows, 0), (span_rows, width))[:2]
    prev = shifted(last, "seq", 1)
    after = shifted(first, "seq", -1)

    outgoing = gather_rows(received, take_rows, prev, masks, weights, cot, filter_taps)
    columns = exchange(outgoing, "seq")
    results = conv_all(columns, tables)
    local = exchange(results, "seq")
    mixed, back, taps = back_rows(
        received, take_rows, give_rows, prev, after, masks, weights, cot, next_cot, local
    )
    returned = exchange(back, "dp")
    taps = total_over(taps, "seq")
    grad_stored = store_grads(select_rows, returned, channels)
    lags = jnp.sum(returned[:, 48:56].astype(F32), axis=0)
    final = jnp.concatenate([lags, taps], axis=0).astype(BF16)
    final = exchange(jnp.broadcast_to(final[None], (dp_count, *final.shape)), "dp").astype(F32)
    grad_filter = final[:, :8].reshape(tok_rows, channels)
    grad_short = jnp.sum(final[:, 8:], axis=0).reshape(3, 3, channels)
    return (mixed[None], grad_stored[None], grad_filter, grad_short)


def solution(mesh):
    return jax.shard_map(
        shards,
        mesh=mesh,
        in_specs=(
            P("dp", "seq", None),
            P(None, "seq", None),
            P(None, "seq"),
            P("dp", "seq"),
            P(),
            P("seq", None),
            P("dp", "seq", None),
        ),
        out_specs=(P("dp", "seq", None), P("dp", "seq", None), P("seq", None), P()),
        check_vma=False,
    )
```

time: 505 us -> 293 us (0.58); the launches traced: 496 us -> 290 us
  waiting for transfers between devices: 203 us -> 107 us
  Pallas kernels: 0 us -> 62.4 us
  matrix products: 52.5 us -> 3.52 us
  blocking collectives: 39.5 us -> 0 us
  other arithmetic: 46.5 us -> 15.5 us
  local copies, waits for them, and re-layouts: 69 us -> 40.2 us
  between operations: 15.2 us -> 2.2 us
  starting transfers between devices: 70.2 us -> 60.2 us
    psum x1 -> x0, waiting for transfers between devices: 131 us -> none  [in_one(): total = lax.psum(line, axis)]
    pallas_call x0 -> x5, Pallas kernels: none -> 62.4 us  [the longest x1 24.6 us: conv_all(): pl.pallas_call(conv_kernel, grid=(17,), in_specs=[whole(16, 384, LANES)]...]
    dot_general x17 -> x2, matrix products: 52.5 us -> 3.52 us  [the longest x1 2.62 us: dot(): return jnp.dot(left, right, preferred_element_type=F32)]
    all_to_all x2 -> x0, blocking collectives: 39.5 us -> none  [the longest x1 20 us: shards(): lax.all_to_all(product, 'seq', split_axis=1, concat_axis=0, tiled=True)]
    ppermute x0 -> x4, waiting for transfers between devices: none -> 36.6 us  [total_over(): lax.ppermute(value, axis, [(i, i ^ step) for i in range(length)])]
    all_to_all x7 -> x5, waiting for transfers between devices: 69.4 us -> 38.8 us  [exchange(): return lax.all_to_all(value, axis, 0, 0, tiled=True)]
    ppermute x3 -> x5, waiting for transfers between devices: 3.13 us -> 31.2 us  [shifted(): return lax.ppermute(value, axis, pairs)]
    all_to_all x7 -> x5, starting transfers between devices: 62.1 us -> 40.1 us  [exchange(): return lax.all_to_all(value, axis, 0, 0, tiled=True)]
  transfers between devices with their start and end apart: 11 -> 14, of which waited for: 7 -> 9; matrix products, arithmetic and copies ran while one was open for 19% -> 14% of each run, Pallas kernels for 0% -> 7%
where the time goes in v1:
time: 293 us; the launch traced here: 290 us
  waiting for transfers between devices  107 us (37%)
  Pallas kernels  62.4 us (21%)
  starting transfers between devices  60.2 us (21%)
  local copies, waits for them, and re-layouts  40.2 us (14%)
  other arithmetic  15.5 us (5%)
  matrix products  3.52 us (1%)
    all_to_all x5, starting transfers between devices, exchange(): return lax.all_to_all(value, axis, 0, 0, tiled=True)  40.1 us
    all_to_all x5, waiting for transfers between devices, exchange(): return lax.all_to_all(value, axis, 0, 0, tiled=True)  38.8 us
    ppermute x4, waiting for transfers between devices, total_over(): lax.ppermute(value, axis, [(i, i ^ step) for i in range(length)])  36.6 us
    ppermute x5, waiting for transfers between devices, shifted(): return lax.ppermute(value, axis, pairs)  31.2 us
    convert_element_type x8, local copies, waits for them, and re-layouts, spread(): return wide.reshape(rows * by, cols * by).astype(BF16)  27.4 us
    pallas_call x1, Pallas kernels, conv_all(): pl.pallas_call(conv_kernel, grid=(17,), in_specs=[whole(16, 384, LANES)]...  24.6 us
    ppermute x5, starting transfers between devices, shifted(): return lax.ppermute(value, axis, pairs)  11.6 us
    pallas_call x1, Pallas kernels, inner_tables(): pl.pallas_call(table_kernel, grid=(17,), in_specs=[whole, whole, pl.Block...  10.8 us
  transfers between devices with their start and end apart: 14, of which 9 were waited for; matrix products, arithmetic and copies ran while one was open for 14% of the time, Pallas kernels for 7%

profile of v1, /device:TPU:1, one launch (start us, length us, event | category | flops | bytes accessed | tf_op | source)
XLA Modules:
  0.0 290.5 jit_solution(4700239161865017643)
XLA Ops:
  7.2 2.6 convolution_convert_fusion
  9.8 8.6 %all-to-all-start = ((bf16[16,16,6144]{2,1,0:T(8,128)(2,1)}), bf16[16,16,6144]{2,1,0:T(8,128)(2,1)}, u32[]{:S(2)}, u32[]{:S(2)}) async-start(bf16[16,16,6144]{2,1,0:T(8,128)(2,1)} %bitcast.56), calls=%async_computation | async-start | bytes 6291456 | tf_op jit(solution)/shard_map/all_to_all | solution.py:27
  19.8 4.2 %collective-permute-start.2 = (s32[2]{0:T(128)S(1)}, s32[2]{0:T(128)S(1)}, u32[]{:S(2)}, u32[]{:S(2)}) collective-permute-start(s32[2]{0:T(128)S(1)} %get-tuple-element.36), channel_id=1, source_target_pairs={{0,1},{1,2},{2,3},{3,4},{4,5},{5,6},{6,7},{7,8},{8,9},{9,10},{10,1... | collective-permute-start | bytes 32 | tf_op jit(solution)/shard_map/ppermute | solution.py:23
  28.0 2.0 convert_element_type.179.take_ref
  30.4 27.6 %all-to-all-done = bf16[16,16,6144]{2,1,0:T(8,128)(2,1)} async-done(((bf16[16,16,6144]{2,1,0:T(8,128)(2,1)}), bf16[16,16,6144]{2,1,0:T(8,128)(2,1)}, u32[]{:S(2)}, u32[]{:S(2)}) %all-to-all-start) | async-done | bytes 3145760 | tf_op jit(solution)/shard_map/all_to_all | solution.py:27
  59.1 3.5 %collective-permute-start = (bf16[2,6144]{1,0:T(2,128)(2,1)S(1)}, bf16[2,6144]{1,0:T(2,128)(2,1)S(1)}, u32[]{:S(2)}, u32[]{:S(2)}) collective-permute-start(bf16[2,6144]{1,0:T(2,128)(2,1)S(1)} %get-tuple-element.19), channel_id=1, source_target_pairs={{0,1},{1,2},{2,3},{3,4},{4,5},{5,6},{6,7},{7,8},{8,9},{9,10},{10,1... | collective-permute-start | bytes 73736 | tf_op jit(solution)/shard_map/ppermute | solution.py:23
  64.1 7.6 %gather_rows.1 = bf16[16,384,128]{2,1,0:T(8,128)(2,1)} custom-call(bf16[256,6144]{1,0:T(8,128)(2,1)} %bitcast.5.k_ref.v_ref.q_ref, bf16[256,6144]{1,0:T(8,128)(2,1)} %bitcast.5.k_ref.v_ref.q_ref, bf16[256,6144]{1,0:T(8,128)(2,1)} %bitcast.5.k_ref.v_ref.q_ref, bf16[128,256]{1,0:T(8,128)(2,1)} %convert_element_type.179.take_ref, bf16[2,6144]{1,0:T(2,128)(2,1)} %copy-done.3, ...), custom_call_target="tpu_custom_call" | custom-call | tf_op jit(solution)/shard_map/gather_rows/pallas_call | solution.py:154
  71.8 9.8 %all-to-all-start.1 = ((bf16[16,384,128]{2,1,0:T(8,128)(2,1)}), bf16[16,384,128]{2,1,0:T(8,128)(2,1)S(1)}, u32[]{:S(2)}, u32[]{:S(2)}) async-start(bf16[16,384,128]{2,1,0:T(8,128)(2,1)} %gather_rows.1), calls=%async_computation.1 | async-start | bytes 3145728 | tf_op jit(solution)/shard_map/all_to_all | solution.py:27
  82.0 1.4 copy.39.col_ref
  83.4 2.7 multiply_convert_fusion.2
  86.1 3.9 %convert_element_type.190.fl_ref = bf16[512,256]{1,0:T(8,128)(2,1)} reshape(bf16[32,16,16,16]{3,2,1,0:T(8,128)(2,1)} %get-tuple-element.22) | data formatting | bytes 524288 | tf_op jit(solution)/shard_map/convert_element_type | solution.py:68
  90.0 3.9 %convert_element_type.188.fh_ref = bf16[512,256]{1,0:T(8,128)(2,1)} reshape(bf16[32,16,16,16]{3,2,1,0:T(8,128)(2,1)} %get-tuple-element.23) | data formatting | bytes 524288 | tf_op jit(solution)/shard_map/convert_element_type | solution.py:68
  93.9 2.8 multiply_convert_fusion
  96.7 5.1 %convert_element_type.194.bl_ref = bf16[256,512]{1,0:T(8,128)(2,1)} reshape(bf16[16,16,32,16]{3,2,1,0:T(8,128)(2,1)} %get-tuple-element.20) | data formatting | bytes 524288 | tf_op jit(solution)/shard_map/convert_element_type | solution.py:68
  101.8 5.1 %convert_element_type.192.bh_ref = bf16[256,512]{1,0:T(8,128)(2,1)} reshape(bf16[16,16,32,16]{3,2,1,0:T(8,128)(2,1)} %get-tuple-element.21) | data formatting | bytes 524288 | tf_op jit(solution)/shard_map/convert_element_type | solution.py:68
  108.8 10.8 %inner_tables.1 = (bf16[17,256,256]{2,1,0:T(8,128)(2,1)}, bf16[17,256,256]{2,1,0:T(8,128)(2,1)}, bf16[17,256,256]{2,1,0:T(8,128)(2,1)}, bf16[17,256,256]{2,1,0:T(8,128)(2,1)}) custom-call(f32[128,128]{1,0:T(8,128)} %get-tuple-element.40.fc_ref, f32[128,128]{1,0:T(8,128)} %get-tuple-element.39.fs_ref, f32[17,2,128]{2,1,0:T(2,128)} %pad_maximum_fusion.1.row_ref, ...), custom_call_target="tpu_custom_call" | custom-call | tf_op jit(solution)/shard_map/inner_tables/pallas_call | solution.py:109
  120.8 24.6 %conv_all.1 = bf16[16,400,128]{2,1,0:T(8,128)(2,1)} custom-call(bf16[16,384,128]{2,1,0:T(8,128)(2,1)} %copy-done.2, bf16[17,256,256]{2,1,0:T(8,128)(2,1)} %get-tuple-element.11.dh_ref, bf16[17,256,256]{2,1,0:T(8,128)(2,1)} %get-tuple-element.12.dl_ref, bf16[17,256,256]{2,1,0:T(8,128)(2,1)} %get-tuple-element.13.eh_ref, ...), custom_call_target="tpu_custom_call" | custom-call | tf_op jit(solution)/shard_map/conv_all/pallas_call | solution.py:248
  145.4 7.5 %all-to-all-start.2 = ((bf16[16,400,128]{2,1,0:T(8,128)(2,1)}), bf16[16,400,128]{2,1,0:T(8,128)(2,1)S(1)}, u32[]{:S(2)}, u32[]{:S(2)}) async-start(bf16[16,400,128]{2,1,0:T(8,128)(2,1)} %conv_all.1), calls=%async_computation.2 | async-start | bytes 3276800 | tf_op jit(solution)/shard_map/all_to_all | solution.py:27
  156.3 3.0 %convert_element_type.182.give_ref = bf16[256,128]{1,0:T(8,128)(2,1)} reshape(bf16[32,8,16,8]{3,2,1,0:T(8,128)(2,1)} %get-tuple-element.26) | data formatting | bytes 131072 | tf_op jit(solution)/shard_map/convert_element_type | solution.py:68
  159.3 30.9 %collective-permute-done.4 = bf16[2,2048]{1,0:T(2,128)(2,1)S(1)} collective-permute-done((bf16[2,2048]{1,0:T(2,128)(2,1)S(1)}, bf16[2,2048]{1,0:T(2,128)(2,1)S(1)}, u32[]{:S(2)}, u32[]{:S(2)}) %collective-permute-start.4) | collective-permute-done | bytes 8224 | tf_op jit(solution)/shard_map/ppermute | solution.py:23
  192.6 10.8 %back_rows.1 = (bf16[128,2048]{1,0:T(8,128)(2,1)}, bf16[16,56,2048]{2,1,0:T(8,128)(2,1)}, f32[9,2048]{1,0:T(8,128)}) custom-call(bf16[256,6144]{1,0:T(8,128)(2,1)} %bitcast.5.k_ref.v_ref.q_ref, bf16[256,6144]{1,0:T(8,128)(2,1)} %bitcast.5.k_ref.v_ref.q_ref, bf16[256,6144]{1,0:T(8,128)(2,1)} %bitcast.5.k_ref.v_ref.q_ref, ...), custom_call_target="tpu_custom_call" | custom-call | tf_op jit(solution)/shard_map/back_rows/pallas_call | solution.py:311
  203.5 6.9 %all-to-all-start.3 = ((bf16[16,56,2048]{2,1,0:T(8,128)(2,1)}), bf16[16,56,2048]{2,1,0:T(8,128)(2,1)}, u32[]{:S(2)}, u32[]{:S(2)}) async-start(bf16[16,56,2048]{2,1,0:T(8,128)(2,1)} %get-tuple-element.16), calls=%async_computation.3 | async-start | bytes 7340032 | tf_op jit(solution)/shard_map/all_to_all | solution.py:27
  210.7 4.6 %collective-permute-done.5 = f32[9,2048]{1,0:T(8,128)S(1)} collective-permute-done((f32[9,2048]{1,0:T(8,128)S(1)}, f32[9,2048]{1,0:T(8,128)S(1)}, u32[]{:S(2)}, u32[]{:S(2)}) %collective-permute-start.5) | collective-permute-done | bytes 73760 | tf_op jit(solution)/shard_map/ppermute | solution.py:372
  215.3 2.7 collective-permute-start.6
  218.0 6.0 %collective-permute-done.6 = f32[9,2048]{1,0:T(8,128)S(1)} collective-permute-done((f32[9,2048]{1,0:T(8,128)S(1)}, f32[9,2048]{1,0:T(8,128)S(1)}, u32[]{:S(2)}, u32[]{:S(2)}) %collective-permute-start.6) | collective-permute-done | bytes 73760 | tf_op jit(solution)/shard_map/ppermute | solution.py:372
  224.0 4.1 %collective-permute-start.7 = (f32[9,2048]{1,0:T(8,128)S(1)}, f32[9,2048]{1,0:T(8,128)S(1)}, u32[]{:S(2)}, u32[]{:S(2)}) collective-permute-start(f32[9,2048]{1,0:T(8,128)S(1)} %add.63), channel_id=1, source_target_pairs={{0,4},{1,5},{2,6},{3,7},{4,0},{5,1},{6,2},{7,3},{8,12},{9,13},{10,... | collective-permute-start | bytes 221192 | tf_op jit(solution)/shard_map/ppermute | solution.py:372
  228.2 7.3 %collective-permute-done.7 = f32[9,2048]{1,0:T(8,128)S(1)} collective-permute-done((f32[9,2048]{1,0:T(8,128)S(1)}, f32[9,2048]{1,0:T(8,128)S(1)}, u32[]{:S(2)}, u32[]{:S(2)}) %collective-permute-start.7) | collective-permute-done | bytes 73760 | tf_op jit(solution)/shard_map/ppermute | solution.py:372
  236.9 18.6 %collective-permute-done.8 = f32[9,2048]{1,0:T(8,128)S(1)} collective-permute-done((f32[9,2048]{1,0:T(8,128)S(1)}, f32[9,2048]{1,0:T(8,128)S(1)}, u32[]{:S(2)}, u32[]{:S(2)}) %collective-permute-start.8) | collective-permute-done | bytes 73760 | tf_op jit(solution)/shard_map/ppermute | solution.py:372
  258.2 7.4 %all-to-all-start.4 = ((bf16[16,17,2048]{2,1,0:T(8,128)(2,1)}), bf16[16,17,2048]{2,1,0:T(8,128)(2,1)S(1)}, u32[]{:S(2)}, u32[]{:S(2)}) async-start(bf16[16,17,2048]{2,1,0:T(8,128)(2,1)} %broadcast_in_dim.8), calls=%async_computation.4 | async-start | bytes 3145728 | tf_op jit(solution)/shard_map/all_to_all | solution.py:27
  265.6 3.3 %convert_element_type.196.select_ref = bf16[128,256]{1,0:T(8,128)(2,1)} reshape(bf16[16,8,32,8]{3,2,1,0:T(8,128)(2,1)} %get-tuple-element.24) | data formatting | bytes 131072 | tf_op jit(solution)/shard_map/convert_element_type | solution.py:68
  268.8 8.5 %store_grads.1 = bf16[128,6144]{1,0:T(8,128)(2,1)} custom-call(bf16[128,256]{1,0:T(8,128)(2,1)} %convert_element_type.196.select_ref, bf16[16,56,2048]{2,1,0:T(8,128)(2,1)} %all-to-all-done.3.in_ref), custom_call_target="tpu_custom_call" | custom-call | tf_op jit(solution)/shard_map/store_grads/pallas_call | solution.py:355
  277.3 10.9 %all-to-all-done.4 = bf16[16,17,2048]{2,1,0:T(8,128)(2,1)S(1)} async-done(((bf16[16,17,2048]{2,1,0:T(8,128)(2,1)}), bf16[16,17,2048]{2,1,0:T(8,128)(2,1)S(1)}, u32[]{:S(2)}, u32[]{:S(2)}) %all-to-all-start.4) | async-done | bytes 1114144 | tf_op jit(solution)/shard_map/all_to_all | solution.py:27
  (83 shorter events, 29.4 us)
Async XLA Ops:
  0.6 6.5 %copy-start = (bf16[1,128,6144]{2,1,0:T(8,128)(2,1)S(1)}, bf16[1,128,6144]{2,1,0:T(8,128)(2,1)}, u32[]{:S(2)}) copy-start(bf16[1,128,6144]{2,1,0:T(8,128)(2,1)} %param.12) | copy-start | bytes 4718596
  9.8 8.6 %copy-start.12 = (s32[1,128]{1,0:T(1,128)S(1)}, s32[1,128]{1,0:T(1,128)}, u32[]{:S(2)}) copy-start(s32[1,128]{1,0:T(1,128)} %param.15) | copy-start | bytes 1540
  9.8 16.1 %copy-start.6 = (f32[3,3,2048]{2,1,0:T(4,128)S(1)}, f32[3,3,2048]{2,1,0:T(4,128)}, u32[]{:S(2)}) copy-start(f32[3,3,2048]{2,1,0:T(4,128)} %param.16) | copy-start | bytes 221188
  9.8 48.3 %all-to-all-start = ((bf16[16,16,6144]{2,1,0:T(8,128)(2,1)}), bf16[16,16,6144]{2,1,0:T(8,128)(2,1)}, u32[]{:S(2)}, u32[]{:S(2)}) async-start(bf16[16,16,6144]{2,1,0:T(8,128)(2,1)} %bitcast.56), calls=%async_computation | async-start | bytes 6291456 | tf_op jit(solution)/shard_map/all_to_all | solution.py:27
  18.5 11.6 %collective-permute-start.3 = (s32[2]{0:T(128)S(1)}, s32[2]{0:T(128)S(1)}, u32[]{:S(2)}, u32[]{:S(2)}) collective-permute-start(s32[2]{0:T(128)S(1)} %get-tuple-element.35), channel_id=1, source_target_pairs={{1,0},{2,1},{3,2},{4,3},{5,4},{6,5},{7,6},{8,7},{9,8},{10,9},{11,1... | collective-permute-start | bytes 32 | tf_op jit(solution)/shard_map/ppermute | solution.py:23
  19.8 10.3 %collective-permute-start.2 = (s32[2]{0:T(128)S(1)}, s32[2]{0:T(128)S(1)}, u32[]{:S(2)}, u32[]{:S(2)}) collective-permute-start(s32[2]{0:T(128)S(1)} %get-tuple-element.36), channel_id=1, source_target_pairs={{0,1},{1,2},{2,3},{3,4},{4,5},{5,6},{6,7},{7,8},{8,9},{9,10},{10,1... | collective-permute-start | bytes 32 | tf_op jit(solution)/shard_map/ppermute | solution.py:23
  59.1 4.5 %collective-permute-start = (bf16[2,6144]{1,0:T(2,128)(2,1)S(1)}, bf16[2,6144]{1,0:T(2,128)(2,1)S(1)}, u32[]{:S(2)}, u32[]{:S(2)}) collective-permute-start(bf16[2,6144]{1,0:T(2,128)(2,1)S(1)} %get-tuple-element.19), channel_id=1, source_target_pairs={{0,1},{1,2},{2,3},{3,4},{4,5},{5,6},{6,7},{7,8},{8,9},{9,10},{10,1... | collective-permute-start | bytes 73736 | tf_op jit(solution)/shard_map/ppermute | solution.py:23
  63.5 0.6 copy-start.3
  71.8 9.8 %copy-start.11 = (s32[17]{0:T(128)S(1)}, s32[17]{0:T(128)}, u32[]{:S(2)}) copy-start(s32[17]{0:T(128)} %constant.62.clone) | copy-start | bytes 208
  71.8 11.6 %copy-start.7 = (f32[32,16]{1,0:T(8,128)S(1)}, f32[32,16]{1,0:T(8,128)}, u32[]{:S(2)}) copy-start(f32[32,16]{1,0:T(8,128)} %constant.64.clone) | copy-start | bytes 6148
  71.8 11.6 %copy-start.8 = (f32[32,16]{1,0:T(8,128)S(1)}, f32[32,16]{1,0:T(8,128)}, u32[]{:S(2)}) copy-start(f32[32,16]{1,0:T(8,128)} %constant.63.clone) | copy-start | bytes 6148
  71.8 47.8 %all-to-all-start.1 = ((bf16[16,384,128]{2,1,0:T(8,128)(2,1)}), bf16[16,384,128]{2,1,0:T(8,128)(2,1)S(1)}, u32[]{:S(2)}, u32[]{:S(2)}) async-start(bf16[16,384,128]{2,1,0:T(8,128)(2,1)} %gather_rows.1), calls=%async_computation.1 | async-start | bytes 3145728 | tf_op jit(solution)/shard_map/all_to_all | solution.py:27
  86.1 7.8 %copy-start.9 = (f32[16,32]{1,0:T(8,128)S(1)}, f32[16,32]{1,0:T(8,128)}, u32[]{:S(2)}) copy-start(f32[16,32]{1,0:T(8,128)} %constant.66.clone) | copy-start | bytes 6148
  86.1 7.8 %copy-start.10 = (f32[16,32]{1,0:T(8,128)S(1)}, f32[16,32]{1,0:T(8,128)}, u32[]{:S(2)}) copy-start(f32[16,32]{1,0:T(8,128)} %constant.65.clone) | copy-start | bytes 6148
  119.6 1.1 copy-start.2
  145.4 45.4 %all-to-all-start.2 = ((bf16[16,400,128]{2,1,0:T(8,128)(2,1)}), bf16[16,400,128]{2,1,0:T(8,128)(2,1)S(1)}, u32[]{:S(2)}, u32[]{:S(2)}) async-start(bf16[16,400,128]{2,1,0:T(8,128)(2,1)} %conv_all.1), calls=%async_computation.2 | async-start | bytes 3276800 | tf_op jit(solution)/shard_map/all_to_all | solution.py:27
  152.9 37.9 %collective-permute-start.1 = (bf16[2,6144]{1,0:T(2,128)(2,1)S(1)}, bf16[2,6144]{1,0:T(2,128)(2,1)S(1)}, u32[]{:S(2)}, u32[]{:S(2)}) collective-permute-start(bf16[2,6144]{1,0:T(2,128)(2,1)S(1)} %get-tuple-element.18), channel_id=1, source_target_pairs={{1,0},{2,1},{3,2},{4,3},{5,4},{6,5},{7,6},{8,7},{9,8},{10,9},{11,1... | collective-permute-start | bytes 73736 | tf_op jit(solution)/shard_map/ppermute | solution.py:23
  155.0 35.2 %collective-permute-start.4 = (bf16[2,2048]{1,0:T(2,128)(2,1)S(1)}, bf16[2,2048]{1,0:T(2,128)(2,1)S(1)}, u32[]{:S(2)}, u32[]{:S(2)}) collective-permute-start(bf16[2,2048]{1,0:T(2,128)(2,1)S(1)} %slice_bitcast_fusion.1), channel_id=1, source_target_pairs={{1,0},{2,1},{3,2},{4,3},{5,4},{6,5},{7,6},{8,7},{9,8},{10,9},{11,1... | collective-permute-start | bytes 24584 | tf_op jit(solution)/shard_map/ppermute | solution.py:23
  190.8 0.6 copy-start.4
  191.4 1.2 copy-start.1
  203.5 6.9 %copy-start.5 = (f32[9,2048]{1,0:T(8,128)S(1)}, f32[9,2048]{1,0:T(8,128)}, u32[]{:S(2)}) copy-start(f32[9,2048]{1,0:T(8,128)} %get-tuple-element.17) | copy-start | bytes 221188
  203.5 52.3 %all-to-all-start.3 = ((bf16[16,56,2048]{2,1,0:T(8,128)(2,1)}), bf16[16,56,2048]{2,1,0:T(8,128)(2,1)}, u32[]{:S(2)}, u32[]{:S(2)}) async-start(bf16[16,56,2048]{2,1,0:T(8,128)(2,1)} %get-tuple-element.16), calls=%async_computation.3 | async-start | bytes 7340032 | tf_op jit(solution)/shard_map/all_to_all | solution.py:27
  210.3 5.0 %collective-permute-start.5 = (f32[9,2048]{1,0:T(8,128)S(1)}, f32[9,2048]{1,0:T(8,128)S(1)}, u32[]{:S(2)}, u32[]{:S(2)}) collective-permute-start(f32[9,2048]{1,0:T(8,128)S(1)} %copy-done.5), channel_id=1, source_target_pairs={{0,1},{1,0},{2,3},{3,2},{4,5},{5,4},{6,7},{7,6},{8,9},{9,8},{10,11... | collective-permute-start | bytes 221192 | tf_op jit(solution)/shard_map/ppermute | solution.py:372
  215.3 8.7 %collective-permute-start.6 = (f32[9,2048]{1,0:T(8,128)S(1)}, f32[9,2048]{1,0:T(8,128)S(1)}, u32[]{:S(2)}, u32[]{:S(2)}) collective-permute-start(f32[9,2048]{1,0:T(8,128)S(1)} %add.62), channel_id=1, source_target_pairs={{0,2},{1,3},{2,0},{3,1},{4,6},{5,7},{6,4},{7,5},{8,10},{9,11},{10,... | collective-permute-start | bytes 221192 | tf_op jit(solution)/shard_map/ppermute | solution.py:372
  224.0 11.5 %collective-permute-start.7 = (f32[9,2048]{1,0:T(8,128)S(1)}, f32[9,2048]{1,0:T(8,128)S(1)}, u32[]{:S(2)}, u32[]{:S(2)}) collective-permute-start(f32[9,2048]{1,0:T(8,128)S(1)} %add.63), channel_id=1, source_target_pairs={{0,4},{1,5},{2,6},{3,7},{4,0},{5,1},{6,2},{7,3},{8,12},{9,13},{10,... | collective-permute-start | bytes 221192 | tf_op jit(solution)/shard_map/ppermute | solution.py:372
  235.5 20.0 %collective-permute-start.8 = (f32[9,2048]{1,0:T(8,128)S(1)}, f32[9,2048]{1,0:T(8,128)S(1)}, u32[]{:S(2)}, u32[]{:S(2)}) collective-permute-start(f32[9,2048]{1,0:T(8,128)S(1)} %add.64), channel_id=1, source_target_pairs={{0,8},{1,9},{2,10},{3,11},{4,12},{5,13},{6,14},{7,15},{8,0},{9,1},... | collective-permute-start | bytes 221192 | tf_op jit(solution)/shard_map/ppermute | solution.py:372
  258.2 30.1 %all-to-all-start.4 = ((bf16[16,17,2048]{2,1,0:T(8,128)(2,1)}), bf16[16,17,2048]{2,1,0:T(8,128)(2,1)S(1)}, u32[]{:S(2)}, u32[]{:S(2)}) async-start(bf16[16,17,2048]{2,1,0:T(8,128)(2,1)} %broadcast_in_dim.8), calls=%async_computation.4 | async-start | bytes 3145728 | tf_op jit(solution)/shard_map/all_to_all | solution.py:27
